TPU v7x, 128 devices: a whole 4x4x4 slice. The times are simulated.
128 devices in a mesh: prow: 8 (over y, core), pcol: 16 (over x, z).
Axes of the slice: x: 4, y: 4, z: 4, core: 2. Of those that a mesh axis runs over, the one named last changes fastest.
Arguments:
- right_sides: bfloat16 [32768, 128], P(('prow', 'pcol')), may hold values from -6 to 6
- factor: bfloat16 [16, 16, 32, 8, 128, 128], P(None, 'pcol', None, 'prow'), may hold values from -0.046875 to 0.046875
- pattern: int32 [16, 16, 32, 8], P(None, 'pcol', None, 'prow'), may hold values 0 or 1
- lower_inverse: bfloat16 [16, 16, 128, 128], P(None, 'pcol'), may hold values from -0.5 to 0.5
- upper_inverse: bfloat16 [16, 16, 128, 128], P(None, 'pcol'), may hold values from -0.5 to 0.5
Outputs:
- solution: bfloat16 [32768, 128], P(('prow', 'pcol'))
All inputs are finite; a program needn't handle non-finite values. No bound on the sum of `pattern` on one device may be relied on, other than what follows from the above.
Results may differ from a plain program's by a relative error of at most 0.02.
Values may be sent and summed in bfloat16 or wider, within the bound.
A program may use at most 128 MiB of HBM per device.

v0:
```python
import jax
import jax.numpy as jnp
from jax import lax
from jax.sharding import PartitionSpec as P


def level_index(index_vals, node_count):
    bounds = (node_count // 2, 3 * node_count // 4, 7 * node_count // 8)
    result = jnp.zeros(index_vals.shape, jnp.int32)
    for edge_val in bounds:
        result = result + (index_vals >= edge_val).astype(jnp.int32)
    return result


def level_sums(
    blocks,
    pattern_loc,
    col_levels,
    solved_all,
    row_id,
    prow_n,
    row_start,
    row_end,
    col_start,
    col_end,
    level_id,
    upward,
):
    if col_end <= col_start:
        return None
    block_size = blocks.shape[2]
    rhs_count = solved_all.shape[2]
    grouped = solved_all.reshape(-1, prow_n, block_size, rhs_count)
    column_vals = lax.dynamic_index_in_dim(grouped, row_id, 1, keepdims=False)[col_start:col_end]
    levels_here = col_levels[col_start:col_end]
    if upward:
        order_mask = levels_here > level_id
    else:
        order_mask = levels_here < level_id
    keep_mask = (pattern_loc[row_start:row_end, col_start:col_end] > 0) & order_mask[None, :]
    masked = jnp.where(
        keep_mask[:, :, None, None],
        blocks[row_start:row_end, col_start:col_end],
        jnp.zeros((), jnp.bfloat16),
    )
    return jnp.einsum("ijab,jbn->ian", masked, column_vals, preferred_element_type=jnp.float32)


def finish_level(partial_value, base_rows, inverse_rows, pcol_n):
    row_count = base_rows.shape[0]
    block_size = base_rows.shape[1]
    rhs_count = base_rows.shape[2]
    if partial_value is None:
        remainder = base_rows
    else:
        summed = lax.psum(partial_value.astype(jnp.bfloat16), "prow").astype(jnp.float32)
        remainder = (base_rows.astype(jnp.float32) - summed).astype(jnp.bfloat16)
    solved = jnp.einsum(
        "iab,ibn->ian", inverse_rows, remainder, preferred_element_type=jnp.float32
    ).astype(jnp.bfloat16)
    gathered = lax.all_gather(solved[:, None], "pcol", axis=1, tiled=True)
    return gathered.reshape(row_count * pcol_n, block_size, rhs_count)


def on_device(right_sides, factor, pattern, lower_inverse, upper_inverse):
    prow_n = lax.axis_size("prow")
    pcol_n = lax.axis_size("pcol")
    row_id = lax.axis_index("prow")
    col_id = lax.axis_index("pcol")
    blocks = factor[:, 0, :, 0]
    pattern_loc = pattern[:, 0, :, 0]
    lower_rows = lower_inverse[:, 0]
    upper_rows = upper_inverse[:, 0]
    row_blocks = blocks.shape[0]
    col_blocks = blocks.shape[1]
    block_size = blocks.shape[2]
    rhs_count = right_sides.shape[1]
    node_count = row_blocks * pcol_n
    everything = lax.all_gather(right_sides, ("prow", "pcol"), axis=0, tiled=True)
    everything = everything.reshape(row_blocks, pcol_n, block_size, rhs_count)
    mine_right = lax.dynamic_index_in_dim(everything, col_id, 1, keepdims=False)
    col_levels = level_index(jnp.arange(col_blocks, dtype=jnp.int32) * prow_n + row_id, node_count)
    bounds = (0, row_blocks // 2, 3 * row_blocks // 4, 7 * row_blocks // 8, row_blocks)
    forward_vals = jnp.zeros((node_count, block_size, rhs_count), jnp.bfloat16)
    for level_id in range(4):
        row_start, row_end = (bounds[level_id], bounds[level_id + 1])
        col_end = min(col_blocks, -(-(row_start * pcol_n) // prow_n))
        partial_value = level_sums(
            blocks,
            pattern_loc,
            col_levels,
            forward_vals,
            row_id,
            prow_n,
            row_start,
            row_end,
            0,
            col_end,
            level_id,
            False,
        )
        solved = finish_level(
            partial_value, mine_right[row_start:row_end], lower_rows[row_start:row_end], pcol_n
        )
        forward_vals = lax.dynamic_update_slice_in_dim(forward_vals, solved, row_start * pcol_n, 0)
    forward_mine = lax.dynamic_index_in_dim(
        forward_vals.reshape(row_blocks, pcol_n, block_size, rhs_count), col_id, 1, keepdims=False
    )
    backward_vals = jnp.zeros((node_count, block_size, rhs_count), jnp.bfloat16)
    for level_id in (3, 2, 1, 0):
        row_start, row_end = (bounds[level_id], bounds[level_id + 1])
        col_start = row_end * pcol_n // prow_n
        partial_value = level_sums(
            blocks,
            pattern_loc,
            col_levels,
            backward_vals,
            row_id,
            prow_n,
            row_start,
            row_end,
            col_start,
            col_blocks,
            level_id,
            True,
        )
        solved = finish_level(
            partial_value, forward_mine[row_start:row_end], upper_rows[row_start:row_end], pcol_n
        )
        backward_vals = lax.dynamic_update_slice_in_dim(
            backward_vals, solved, row_start * pcol_n, 0
        )
    out_rows = right_sides.shape[0]
    device_id = row_id * pcol_n + col_id
    flat = backward_vals.reshape(node_count * block_size, rhs_count)
    return lax.dynamic_slice_in_dim(flat, device_id * out_rows, out_rows, 0)


def solution(mesh):
    placed = (
        P(("prow", "pcol"), None),
        P(None, "pcol", None, "prow", None, None),
        P(None, "pcol", None, "prow"),
        P(None, "pcol", None, None),
        P(None, "pcol", None, None),
    )
    return jax.shard_map(
        on_device, mesh=mesh, in_specs=placed, out_specs=P(("prow", "pcol"), None), check_vma=False
    )
```

profile of v0, /device:TPU:0, one launch (start us, length us, event | category | flops | bytes accessed | tf_op | source)
XLA Modules:
  0.0 902.8 jit_solution(18157509265006647587)
XLA Ops:
  7.3 75.4 %all-gather.18.cloned.1.call-done = bf16[32768,128]{1,0:T(8,128)(2,1)} async-done(((bf16[256,128]{1,0:T(8,128)(2,1)}), bf16[32768,128]{1,0:T(8,128)(2,1)}) %all-gather.18.cloned.1.call-update) | async-done | bytes 8388624 | tf_op jit(solution)/shard_map/all_gather | solution.py:79
  85.7 53.7 %all-gather.20.cloned.1.call-done = bf16[8,2048,128]{1,2,0:T(8,128)(2,1)} async-done(((bf16[8,128,128]{1,2,0:T(8,128)(2,1)}), bf16[8,2048,128]{1,2,0:T(8,128)(2,1)}) %all-gather.20.cloned.1.call-update) | async-done | bytes 4194320 | tf_op jit(solution)/shard_map/all_gather | solution.py:61
  139.4 6.5 copy.16
  145.9 4.1 dynamic_update_slice.24
  150.0 3.2 copy-done
  153.2 3.1 fusion.15
  157.5 58.3 %all-reduce.9.cloned.1.call-done = bf16[4,128,128]{1,2,0:T(8,128)(2,1)} async-done(((bf16[4,128,128]{1,2,0:T(8,128)(2,1)}), bf16[4,128,128]{1,2,0:T(8,128)(2,1)}) %all-reduce.9.cloned.1.call-update) | async-done | bytes 131088 | tf_op jit(solution)/shard_map/psum | solution.py:56
  217.7 46.2 %all-gather.22.cloned.1.call-done = bf16[4,2048,128]{1,2,0:T(8,128)(2,1)} async-done(((bf16[4,128,128]{1,2,0:T(8,128)(2,1)}), bf16[4,2048,128]{1,2,0:T(8,128)(2,1)}) %all-gather.22.cloned.1.call-update) | async-done | bytes 2097168 | tf_op jit(solution)/shard_map/all_gather | solution.py:61
  272.6 58.2 %all-reduce.11.cloned.1.call-done = bf16[2,128,128]{1,2,0:T(8,128)(2,1)} async-done(((bf16[2,128,128]{1,2,0:T(8,128)(2,1)}), bf16[2,128,128]{1,2,0:T(8,128)(2,1)}) %all-reduce.11.cloned.1.call-update) | async-done | bytes 65552 | tf_op jit(solution)/shard_map/psum | solution.py:56
  332.5 42.4 %all-gather.24.cloned.1.call-done = bf16[2,2048,128]{1,2,0:T(8,128)(2,1)} async-done(((bf16[2,128,128]{1,2,0:T(8,128)(2,1)}), bf16[2,2048,128]{1,2,0:T(8,128)(2,1)}) %all-gather.24.cloned.1.call-update) | async-done | bytes 1048592 | tf_op jit(solution)/shard_map/all_gather | solution.py:61
  377.6 3.2 fusion.20
  381.0 59.0 %all-reduce.13.cloned.1.call-done = bf16[2,128,128]{1,2,0:T(8,128)(2,1)} async-done(((bf16[2,128,128]{1,2,0:T(8,128)(2,1)}), bf16[2,128,128]{1,2,0:T(8,128)(2,1)}) %all-reduce.13.cloned.1.call-update) | async-done | bytes 65552 | tf_op jit(solution)/shard_map/psum | solution.py:56
  441.7 42.6 %all-gather.26.cloned.1.call-done = bf16[2,2048,128]{1,2,0:T(8,128)(2,1)} async-done(((bf16[2,128,128]{1,2,0:T(8,128)(2,1)}), bf16[2,2048,128]{1,2,0:T(8,128)(2,1)}) %all-gather.26.cloned.1.call-update) | async-done | bytes 1048592 | tf_op jit(solution)/shard_map/all_gather | solution.py:61
  488.9 42.5 %all-gather.28.cloned.1.call-done = bf16[2,2048,128]{1,2,0:T(8,128)(2,1)} async-done(((bf16[2,128,128]{1,2,0:T(8,128)(2,1)}), bf16[2,2048,128]{1,2,0:T(8,128)(2,1)}) %all-gather.28.cloned.1.call-update) | async-done | bytes 1048592 | tf_op jit(solution)/shard_map/all_gather | solution.py:61
  533.0 5.3 dynamic_update_slice.28
  541.3 58.2 %all-reduce.15.cloned.1.call-done = bf16[2,128,128]{1,2,0:T(8,128)(2,1)} async-done(((bf16[2,128,128]{1,2,0:T(8,128)(2,1)}), bf16[2,128,128]{1,2,0:T(8,128)(2,1)}) %all-reduce.15.cloned.1.call-update) | async-done | bytes 65552 | tf_op jit(solution)/shard_map/psum | solution.py:56
  601.3 42.4 %all-gather.30.cloned.1.call-done = bf16[2,2048,128]{1,2,0:T(8,128)(2,1)} async-done(((bf16[2,128,128]{1,2,0:T(8,128)(2,1)}), bf16[2,2048,128]{1,2,0:T(8,128)(2,1)}) %all-gather.30.cloned.1.call-update) | async-done | bytes 1048592 | tf_op jit(solution)/shard_map/all_gather | solution.py:61
  650.0 58.2 %all-reduce.17.cloned.1.call-done = bf16[4,128,128]{1,2,0:T(8,128)(2,1)} async-done(((bf16[4,128,128]{1,2,0:T(8,128)(2,1)}), bf16[4,128,128]{1,2,0:T(8,128)(2,1)}) %all-reduce.17.cloned.1.call-update) | async-done | bytes 131088 | tf_op jit(solution)/shard_map/psum | solution.py:56
  710.1 46.3 %all-gather.32.cloned.1.call-done = bf16[4,2048,128]{1,2,0:T(8,128)(2,1)} async-done(((bf16[4,128,128]{1,2,0:T(8,128)(2,1)}), bf16[4,2048,128]{1,2,0:T(8,128)(2,1)}) %all-gather.32.cloned.1.call-update) | async-done | bytes 2097168 | tf_op jit(solution)/shard_map/all_gather | solution.py:61
  761.0 4.6 fusion.10
  766.8 58.6 %all-reduce.19.cloned.1.call-done = bf16[8,128,128]{1,2,0:T(8,128)(2,1)} async-done(((bf16[8,128,128]{1,2,0:T(8,128)(2,1)}), bf16[8,128,128]{1,2,0:T(8,128)(2,1)}) %all-reduce.19.cloned.1.call-update) | async-done | bytes 262160 | tf_op jit(solution)/shard_map/psum | solution.py:56
  827.4 56.1 %all-gather.34.cloned.1.call-done = bf16[8,2048,128]{1,2,0:T(8,128)(2,1)} async-done(((bf16[8,128,128]{1,2,0:T(8,128)(2,1)}), bf16[8,2048,128]{1,2,0:T(8,128)(2,1)}) %all-gather.34.cloned.1.call-update) | async-done | bytes 4194320 | tf_op jit(solution)/shard_map/all_gather | solution.py:61
  883.5 6.5 copy.31
  890.0 4.7 constant_dynamic-update-slice_fusion
  (83 shorter events, 49.8 us)
Async XLA Ops:
  6.5 76.2 %all-gather.18.cloned.1.call-start = ((), (), s32[]{:S(2)}) async-start(), calls=%async_computation | async-start | bytes 8454144 | tf_op jit(solution)/shard_map/all_gather | solution.py:79
  7.3 132.1 %all-gather.20.cloned.1.call-start = ((), (), s32[]{:S(2)}) async-start(), calls=%async_computation.7 | async-start | bytes 4456448 | tf_op jit(solution)/shard_map/all_gather | solution.py:61
  84.8 131.0 %all-reduce.9.cloned.1.call-start = ((), (), s32[]{:S(2)}) async-start(), calls=%async_computation.1 | async-start | bytes 262144 | tf_op jit(solution)/shard_map/psum | solution.py:56
  145.9 69.9 %copy-start.1 = (bf16[16,1,128,128]{3,2,1,0:T(8,128)(2,1)S(1)}, bf16[16,1,128,128]{3,2,1,0:T(8,128)(2,1)}, u32[]{:S(2)}) copy-start(bf16[16,1,128,128]{3,2,1,0:T(8,128)(2,1)} %param.8) | copy-start | bytes 1572868
  145.9 71.8 %copy-start.3 = (s32[16,1,32,1]{2,3,1,0:T(1,128)S(1)}, s32[16,1,32,1]{2,3,1,0:T(1,128)}, u32[]{:S(2)}) copy-start(s32[16,1,32,1]{2,3,1,0:T(1,128)} %param.7) | copy-start | bytes 6148
  150.0 3.2 copy-start
  156.4 107.5 %all-gather.22.cloned.1.call-start = ((), (), s32[]{:S(2)}) async-start(), calls=%async_computation.8 | async-start | bytes 2228224 | tf_op jit(solution)/shard_map/all_gather | solution.py:61
  217.6 113.2 %all-reduce.11.cloned.1.call-start = ((), (), s32[]{:S(2)}) async-start(), calls=%async_computation.2 | async-start | bytes 131072 | tf_op jit(solution)/shard_map/psum | solution.py:56
  268.4 218.5 %copy-start.2 = (bf16[16,1,128,128]{3,2,1,0:T(8,128)(2,1)S(1)}, bf16[16,1,128,128]{3,2,1,0:T(8,128)(2,1)}, u32[]{:S(2)}) copy-start(bf16[16,1,128,128]{3,2,1,0:T(8,128)(2,1)} %param.9) | copy-start | bytes 1572868
  271.5 103.4 %all-gather.24.cloned.1.call-start = ((), (), s32[]{:S(2)}) async-start(), calls=%async_computation.9 | async-start | bytes 1114112 | tf_op jit(solution)/shard_map/all_gather | solution.py:61
  332.4 107.6 %all-reduce.13.cloned.1.call-start = ((), (), s32[]{:S(2)}) async-start(), calls=%async_computation.3 | async-start | bytes 131072 | tf_op jit(solution)/shard_map/psum | solution.py:56
  380.8 103.5 %all-gather.26.cloned.1.call-start = ((), (), s32[]{:S(2)}) async-start(), calls=%async_computation.10 | async-start | bytes 1114112 | tf_op jit(solution)/shard_map/all_gather | solution.py:61
  441.7 89.7 %all-gather.28.cloned.1.call-start = ((), (), s32[]{:S(2)}) async-start(), calls=%async_computation.11 | async-start | bytes 1114112 | tf_op jit(solution)/shard_map/all_gather | solution.py:61
  488.7 110.8 %all-reduce.15.cloned.1.call-start = ((), (), s32[]{:S(2)}) async-start(), calls=%async_computation.4 | async-start | bytes 131072 | tf_op jit(solution)/shard_map/psum | solution.py:56
  540.2 103.5 %all-gather.30.cloned.1.call-start = ((), (), s32[]{:S(2)}) async-start(), calls=%async_computation.12 | async-start | bytes 1114112 | tf_op jit(solution)/shard_map/all_gather | solution.py:61
  601.1 107.1 %all-reduce.17.cloned.1.call-start = ((), (), s32[]{:S(2)}) async-start(), calls=%async_computation.5 | async-start | bytes 262144 | tf_op jit(solution)/shard_map/psum | solution.py:56
  648.9 107.6 %all-gather.32.cloned.1.call-start = ((), (), s32[]{:S(2)}) async-start(), calls=%async_computation.13 | async-start | bytes 2228224 | tf_op jit(solution)/shard_map/all_gather | solution.py:61
  710.0 115.4 %all-reduce.19.cloned.1.call-start = ((), (), s32[]{:S(2)}) async-start(), calls=%async_computation.6 | async-start | bytes 524288 | tf_op jit(solution)/shard_map/psum | solution.py:56
  765.6 117.9 %all-gather.34.cloned.1.call-start = ((), (), s32[]{:S(2)}) async-start(), calls=%async_computation.14 | async-start | bytes 4456448 | tf_op jit(solution)/shard_map/all_gather | solution.py:61
Sparse Core Ops, SparseCore 0:
  10.5 72.1 all-gather.17
  84.9 54.4 all-gather.19
  156.5 59.2 all-reduce.8
  217.8 46.0 all-gather.21
  271.6 59.1 all-reduce.10
  332.7 42.1 all-gather.23
  380.9 59.0 all-reduce.12
  442.1 42.1 all-gather.25
  488.8 42.5 all-gather.27
  540.4 59.0 all-reduce.14
  601.6 42.1 all-gather.29
  649.0 59.1 all-reduce.16
  710.3 46.0 all-gather.31
  765.7 59.6 all-reduce.18
  827.5 55.9 all-gather.33
where the time goes:
time: 904 us; the launch traced here: 903 us
  waiting for transfers between devices  799 us (88%)
  local copies, waits for them, and re-layouts  55.9 us (6%)
  matrix products  32.5 us (4%)
  between operations  13.5 us (1%)
    all_gather x8, waiting for transfers between devices, finish_level(): gathered = lax.all_gather(solved[:, None], 'pcol', axis=1, tiled=True)  372 us
    psum x6, waiting for transfers between devices, finish_level(): lax.psum(partial_value.astype(jnp.bfloat16), 'prow').astype(jnp.float32)  351 us
    all_gather x1, waiting for transfers between devices, on_device(): lax.all_gather(right_sides, ('prow', 'pcol'), axis=0, tiled=True)  75.4 us
    all_gather x8, local copies, waits for them, and re-layouts, finish_level(): gathered = lax.all_gather(solved[:, None], 'pcol', axis=1, tiled=True)  25.4 us
    dot_general x6, matrix products, level_sums(): jnp.einsum('ijab,jbn->ian', masked, column_vals, preferred_element_type=j...  18.3 us
  transfers between devices with their start and end apart: 15, of which 15 were waited for; matrix products, arithmetic and copies ran while one was open for 1% of the time, Pallas kernels for 0%

commit v1 on v0

--- a/solution.py
+++ b/solution.py
@@ -76,7 +76,12 @@
     block_size = blocks.shape[2]
     rhs_count = right_sides.shape[1]
     node_count = row_blocks * pcol_n
-    everything = lax.all_gather(right_sides, ("prow", "pcol"), axis=0, tiled=True)
+    everything = jnp.concatenate(
+        lax.all_to_all(
+            jnp.stack(lax.axis_size(("prow", "pcol")) * [right_sides], 0), ("prow", "pcol"), 0, 0
+        ),
+        0,
+    )
     everything = everything.reshape(row_blocks, pcol_n, block_size, rhs_count)
     mine_right = lax.dynamic_index_in_dim(everything, col_id, 1, keepdims=False)
     col_levels = level_index(jnp.arange(col_blocks, dtype=jnp.int32) * prow_n + row_id, node_count)

time: 904 us -> 948 us (1.049)
  waiting for transfers between devices: 799 us -> 826 us
  starting transfers between devices: 0.58 us -> 12.5 us
    all_to_all x0 -> x1, waiting for transfers between devices: none -> 99.9 us  [on_device(): lax.all_to_all(jnp.stack(lax.axis_size(('prow', 'pcol')) * [right_sides],...]
    all_gather x1 -> x0, waiting for transfers between devices: 75.4 us -> none  [on_device(): lax.all_gather(right_sides, ('prow', 'pcol'), axis=0, tiled=True)]
    all_to_all x0 -> x1, starting transfers between devices: none -> 11.7 us  [on_device(): lax.all_to_all(jnp.stack(lax.axis_size(('prow', 'pcol')) * [right_sides],...]
where the time goes in v1:
time: 948 us; the launch traced here: 947 us
  waiting for transfers between devices  826 us (87%)
  local copies, waits for them, and re-layouts  62 us (7%)
  matrix products  32.4 us (3%)
  between operations  13.5 us (1%)
  starting transfers between devices  12.5 us (1%)
    all_gather x8, waiting for transfers between devices, finish_level(): gathered = lax.all_gather(solved[:, None], 'pcol', axis=1, tiled=True)  376 us
    psum x6, waiting for transfers between devices, finish_level(): lax.psum(partial_value.astype(jnp.bfloat16), 'prow').astype(jnp.float32)  351 us
    all_to_all x1, waiting for transfers between devices, on_device(): lax.all_to_all(jnp.stack(lax.axis_size(('prow', 'pcol')) * [right_sides],...  99.9 us
    all_gather x8, local copies, waits for them, and re-layouts, finish_level(): gathered = lax.all_gather(solved[:, None], 'pcol', axis=1, tiled=True)  25.5 us
  transfers between devices with their start and end apart: 15, of which 15 were waited for; matrix products, arithmetic and copies ran while one was open for 1% of the time, Pallas kernels for 0%

profile of v1, /device:TPU:0, one launch (start us, length us, event | category | flops | bytes accessed | tf_op | source)
XLA Modules:
  0.0 947.0 jit_solution(15998056923002841139)
XLA Ops:
  6.5 6.2 stack.2
  12.7 11.7 %all-to-all-start = ((bf16[128,256,128]{2,1,0:T(8,128)(2,1)}), bf16[128,256,128]{2,1,0:T(8,128)(2,1)}, u32[]{:S(2)}, u32[]{:S(2)}) async-start(bf16[128,256,128]{2,1,0:T(8,128)(2,1)} %stack.2), calls=%async_computation | async-start | bytes 16777216 | tf_op jit(solution)/shard_map/all_to_all | solution.py:80
  24.5 99.9 %all-to-all-done = bf16[128,256,128]{2,1,0:T(8,128)(2,1)} async-done(((bf16[128,256,128]{2,1,0:T(8,128)(2,1)}), bf16[128,256,128]{2,1,0:T(8,128)(2,1)}, u32[]{:S(2)}, u32[]{:S(2)}) %all-to-all-start) | async-done | bytes 8388640 | tf_op jit(solution)/shard_map/all_to_all | solution.py:80
  126.5 57.3 %all-gather.17.cloned.1.call-done = bf16[8,2048,128]{1,2,0:T(8,128)(2,1)} async-done(((bf16[8,128,128]{1,2,0:T(8,128)(2,1)}), bf16[8,2048,128]{1,2,0:T(8,128)(2,1)}) %all-gather.17.cloned.1.call-update) | async-done | bytes 4194320 | tf_op jit(solution)/shard_map/all_gather | solution.py:61
  183.8 6.5 copy.16
  190.3 4.1 dynamic_update_slice.24
  194.3 3.2 copy-done
  201.8 58.3 %all-reduce.9.cloned.1.call-done = bf16[4,128,128]{1,2,0:T(8,128)(2,1)} async-done(((bf16[4,128,128]{1,2,0:T(8,128)(2,1)}), bf16[4,128,128]{1,2,0:T(8,128)(2,1)}) %all-reduce.9.cloned.1.call-update) | async-done | bytes 131088 | tf_op jit(solution)/shard_map/psum | solution.py:56
  262.0 46.4 %all-gather.19.cloned.1.call-done = bf16[4,2048,128]{1,2,0:T(8,128)(2,1)} async-done(((bf16[4,128,128]{1,2,0:T(8,128)(2,1)}), bf16[4,2048,128]{1,2,0:T(8,128)(2,1)}) %all-gather.19.cloned.1.call-update) | async-done | bytes 2097168 | tf_op jit(solution)/shard_map/all_gather | solution.py:61
  317.0 58.2 %all-reduce.11.cloned.1.call-done = bf16[2,128,128]{1,2,0:T(8,128)(2,1)} async-done(((bf16[2,128,128]{1,2,0:T(8,128)(2,1)}), bf16[2,128,128]{1,2,0:T(8,128)(2,1)}) %all-reduce.11.cloned.1.call-update) | async-done | bytes 65552 | tf_op jit(solution)/shard_map/psum | solution.py:56
  377.0 42.4 %all-gather.21.cloned.1.call-done = bf16[2,2048,128]{1,2,0:T(8,128)(2,1)} async-done(((bf16[2,128,128]{1,2,0:T(8,128)(2,1)}), bf16[2,2048,128]{1,2,0:T(8,128)(2,1)}) %all-gather.21.cloned.1.call-update) | async-done | bytes 1048592 | tf_op jit(solution)/shard_map/all_gather | solution.py:61
  425.5 59.0 %all-reduce.13.cloned.1.call-done = bf16[2,128,128]{1,2,0:T(8,128)(2,1)} async-done(((bf16[2,128,128]{1,2,0:T(8,128)(2,1)}), bf16[2,128,128]{1,2,0:T(8,128)(2,1)}) %all-reduce.13.cloned.1.call-update) | async-done | bytes 65552 | tf_op jit(solution)/shard_map/psum | solution.py:56
  486.2 42.6 %all-gather.23.cloned.1.call-done = bf16[2,2048,128]{1,2,0:T(8,128)(2,1)} async-done(((bf16[2,128,128]{1,2,0:T(8,128)(2,1)}), bf16[2,2048,128]{1,2,0:T(8,128)(2,1)}) %all-gather.23.cloned.1.call-update) | async-done | bytes 1048592 | tf_op jit(solution)/shard_map/all_gather | solution.py:61
  533.4 42.5 %all-gather.25.cloned.1.call-done = bf16[2,2048,128]{1,2,0:T(8,128)(2,1)} async-done(((bf16[2,128,128]{1,2,0:T(8,128)(2,1)}), bf16[2,2048,128]{1,2,0:T(8,128)(2,1)}) %all-gather.25.cloned.1.call-update) | async-done | bytes 1048592 | tf_op jit(solution)/shard_map/all_gather | solution.py:61
  577.4 5.3 dynamic_update_slice.28
  585.7 58.2 %all-reduce.15.cloned.1.call-done = bf16[2,128,128]{1,2,0:T(8,128)(2,1)} async-done(((bf16[2,128,128]{1,2,0:T(8,128)(2,1)}), bf16[2,128,128]{1,2,0:T(8,128)(2,1)}) %all-reduce.15.cloned.1.call-update) | async-done | bytes 65552 | tf_op jit(solution)/shard_map/psum | solution.py:56
  645.8 42.3 %all-gather.27.cloned.1.call-done = bf16[2,2048,128]{1,2,0:T(8,128)(2,1)} async-done(((bf16[2,128,128]{1,2,0:T(8,128)(2,1)}), bf16[2,2048,128]{1,2,0:T(8,128)(2,1)}) %all-gather.27.cloned.1.call-update) | async-done | bytes 1048592 | tf_op jit(solution)/shard_map/all_gather | solution.py:61
  694.3 58.2 %all-reduce.17.cloned.1.call-done = bf16[4,128,128]{1,2,0:T(8,128)(2,1)} async-done(((bf16[4,128,128]{1,2,0:T(8,128)(2,1)}), bf16[4,128,128]{1,2,0:T(8,128)(2,1)}) %all-reduce.17.cloned.1.call-update) | async-done | bytes 131088 | tf_op jit(solution)/shard_map/psum | solution.py:56
  754.6 46.0 %all-gather.29.cloned.1.call-done = bf16[4,2048,128]{1,2,0:T(8,128)(2,1)} async-done(((bf16[4,128,128]{1,2,0:T(8,128)(2,1)}), bf16[4,2048,128]{1,2,0:T(8,128)(2,1)}) %all-gather.29.cloned.1.call-update) | async-done | bytes 2097168 | tf_op jit(solution)/shard_map/all_gather | solution.py:61
  805.2 4.6 fusion.10
  811.0 58.6 %all-reduce.19.cloned.1.call-done = bf16[8,128,128]{1,2,0:T(8,128)(2,1)} async-done(((bf16[8,128,128]{1,2,0:T(8,128)(2,1)}), bf16[8,128,128]{1,2,0:T(8,128)(2,1)}) %all-reduce.19.cloned.1.call-update) | async-done | bytes 262160 | tf_op jit(solution)/shard_map/psum | solution.py:56
  871.6 56.1 %all-gather.31.cloned.1.call-done = bf16[8,2048,128]{1,2,0:T(8,128)(2,1)} async-done(((bf16[8,128,128]{1,2,0:T(8,128)(2,1)}), bf16[8,2048,128]{1,2,0:T(8,128)(2,1)}) %all-gather.31.cloned.1.call-update) | async-done | bytes 4194320 | tf_op jit(solution)/shard_map/all_gather | solution.py:61
  927.7 6.5 copy.31
  934.2 4.7 constant_dynamic-update-slice_fusion
  (83 shorter events, 54.9 us)
Async XLA Ops:
  12.7 111.6 %copy-start.1 = (bf16[16,1,128,128]{3,2,1,0:T(8,128)(2,1)S(1)}, bf16[16,1,128,128]{3,2,1,0:T(8,128)(2,1)}, u32[]{:S(2)}) copy-start(bf16[16,1,128,128]{3,2,1,0:T(8,128)(2,1)} %param.8) | copy-start | bytes 1572868
  12.7 113.8 %copy-start.3 = (s32[16,1,32,1]{2,3,1,0:T(1,128)S(1)}, s32[16,1,32,1]{2,3,1,0:T(1,128)}, u32[]{:S(2)}) copy-start(s32[16,1,32,1]{2,3,1,0:T(1,128)} %param.7) | copy-start | bytes 6148
  12.7 111.6 %all-to-all-start = ((bf16[128,256,128]{2,1,0:T(8,128)(2,1)}), bf16[128,256,128]{2,1,0:T(8,128)(2,1)}, u32[]{:S(2)}, u32[]{:S(2)}) async-start(bf16[128,256,128]{2,1,0:T(8,128)(2,1)} %stack.2), calls=%async_computation | async-start | bytes 16777216 | tf_op jit(solution)/shard_map/all_to_all | solution.py:80
  24.4 159.4 %all-gather.17.cloned.1.call-start = ((), (), s32[]{:S(2)}) async-start(), calls=%async_computation.7 | async-start | bytes 4456448 | tf_op jit(solution)/shard_map/all_gather | solution.py:61
  126.4 133.8 %all-reduce.9.cloned.1.call-start = ((), (), s32[]{:S(2)}) async-start(), calls=%async_computation.1 | async-start | bytes 262144 | tf_op jit(solution)/shard_map/psum | solution.py:56
  194.3 3.2 copy-start
  200.7 107.7 %all-gather.19.cloned.1.call-start = ((), (), s32[]{:S(2)}) async-start(), calls=%async_computation.8 | async-start | bytes 2228224 | tf_op jit(solution)/shard_map/all_gather | solution.py:61
  261.9 113.3 %all-reduce.11.cloned.1.call-start = ((), (), s32[]{:S(2)}) async-start(), calls=%async_computation.2 | async-start | bytes 131072 | tf_op jit(solution)/shard_map/psum | solution.py:56
  312.9 218.6 %copy-start.2 = (bf16[16,1,128,128]{3,2,1,0:T(8,128)(2,1)S(1)}, bf16[16,1,128,128]{3,2,1,0:T(8,128)(2,1)}, u32[]{:S(2)}) copy-start(bf16[16,1,128,128]{3,2,1,0:T(8,128)(2,1)} %param.9) | copy-start | bytes 1572868
  316.0 103.4 %all-gather.21.cloned.1.call-start = ((), (), s32[]{:S(2)}) async-start(), calls=%async_computation.9 | async-start | bytes 1114112 | tf_op jit(solution)/shard_map/all_gather | solution.py:61
  376.9 107.6 %all-reduce.13.cloned.1.call-start = ((), (), s32[]{:S(2)}) async-start(), calls=%async_computation.3 | async-start | bytes 131072 | tf_op jit(solution)/shard_map/psum | solution.py:56
  425.3 103.5 %all-gather.23.cloned.1.call-start = ((), (), s32[]{:S(2)}) async-start(), calls=%async_computation.10 | async-start | bytes 1114112 | tf_op jit(solution)/shard_map/all_gather | solution.py:61
  486.1 89.7 %all-gather.25.cloned.1.call-start = ((), (), s32[]{:S(2)}) async-start(), calls=%async_computation.11 | async-start | bytes 1114112 | tf_op jit(solution)/shard_map/all_gather | solution.py:61
  533.2 110.7 %all-reduce.15.cloned.1.call-start = ((), (), s32[]{:S(2)}) async-start(), calls=%async_computation.4 | async-start | bytes 131072 | tf_op jit(solution)/shard_map/psum | solution.py:56
  584.7 103.3 %all-gather.27.cloned.1.call-start = ((), (), s32[]{:S(2)}) async-start(), calls=%async_computation.12 | async-start | bytes 1114112 | tf_op jit(solution)/shard_map/all_gather | solution.py:61
  645.6 107.0 %all-reduce.17.cloned.1.call-start = ((), (), s32[]{:S(2)}) async-start(), calls=%async_computation.5 | async-start | bytes 262144 | tf_op jit(solution)/shard_map/psum | solution.py:56
  693.2 107.4 %all-gather.29.cloned.1.call-start = ((), (), s32[]{:S(2)}) async-start(), calls=%async_computation.13 | async-start | bytes 2228224 | tf_op jit(solution)/shard_map/all_gather | solution.py:61
  754.3 115.3 %all-reduce.19.cloned.1.call-start = ((), (), s32[]{:S(2)}) async-start(), calls=%async_computation.6 | async-start | bytes 524288 | tf_op jit(solution)/shard_map/psum | solution.py:56
  809.8 117.9 %all-gather.31.cloned.1.call-start = ((), (), s32[]{:S(2)}) async-start(), calls=%async_computation.14 | async-start | bytes 4456448 | tf_op jit(solution)/shard_map/all_gather | solution.py:61
Sparse Core Ops, SparseCore 0:
  126.5 57.2 all-gather.16
  200.8 59.2 all-reduce.8
  262.3 46.0 all-gather.18
  316.1 59.1 all-reduce.10
  377.2 42.1 all-gather.20
  425.4 59.0 all-reduce.12
  486.6 42.1 all-gather.22
  533.3 42.5 all-gather.24
  584.8 59.0 all-reduce.14
  645.9 42.1 all-gather.26
  693.3 59.1 all-reduce.16
  754.5 46.0 all-gather.28
  809.9 59.6 all-reduce.18
  871.7 55.9 all-gather.30
